TPU v7x, 256 devices: a whole 4x4x8 slice. The times are simulated.
256 devices in a mesh: ty: 16 (over x_hi, y, core), tx: 16 (over z, x_lo).
Axes of the slice: x: 4 (x_hi: 2, x_lo: 2; x = x_hi * 2 + x_lo), y: 4, z: 8, core: 2. Of those that a mesh axis runs over, the one named last changes fastest.
Arguments:
- object_slices: float32 [2, 2, 2048, 2048], P(None, None, 'ty', 'tx'), may hold values from -5 to 5
- probe: float32 [4, 2, 128, 128], replicated, may hold values from -4 to 4
- measured: float32 [16, 16, 4, 128, 128], P('ty', 'tx'), may hold values from 0 to 2
- offsets: int32 [2, 16, 16, 4], P(None, 'ty', 'tx'), may hold values from 0 to 127, as said below
- counts: int32 [16, 16], P('ty', 'tx'), may hold values from 1 to 4, as said below
Outputs:
- object_grad: float32 [2, 2, 2048, 2048], P(None, None, 'ty', 'tx')
- probe_grad: float32 [4, 2, 128, 128], replicated
Inputs may be any that keep to these rules, and one draw needn't show every extreme that they name: `counts`: each tile has 1 to 4 live slots, and some tile has all 4 live. Every window lies inside the object: in the last tile row (column) the row (column) offset is at most 0. Slot 0 of every tile sits at the largest row and column offsets that its tile allows.
All inputs are finite; a program needn't handle non-finite values.
Results may differ from a plain program's by a relative error of at most 0.0003.
Values sent between devices are 32-bit elements; how exact they have to be, the bound alone decides.
A program may use at most 64 MiB of HBM per device.

v0:
```python
import ml_dtypes
import numpy as np

import jax
import jax.numpy as jnp
from jax import lax
from jax.experimental import pallas as pl
from jax.experimental.pallas import tpu as pltpu
from jax.sharding import PartitionSpec as P

W = 128
MODES = 4
SLOTS = 4
F32 = jnp.float32
BF16 = jnp.bfloat16


def tables():
    k = np.arange(W)
    f1 = np.exp(-2j * np.pi * (np.outer(k, k) % W) / W) / np.sqrt(W)
    freq = (k + W // 2) % W - W // 2
    h = np.exp(-2j * np.pi * (freq * freq % (4 * W)) / (4 * W))
    a = (np.conj(f1) * h[None, :]) @ f1
    out = []
    for m in (a, f1):
        right = np.block([[m.real, m.imag], [-m.imag, m.real]])
        for t in (right, right.T):
            hi = t.astype(ml_dtypes.bfloat16)
            lo = (t - hi.astype(np.float64)).astype(ml_dtypes.bfloat16)
            out.append(np.stack([hi, lo]))
    return np.stack(out)


def split(x):
    hi = x.astype(BF16)
    return hi, (x - hi.astype(F32)).astype(BF16)


def dot(a, b):
    return jnp.dot(a, b, preferred_element_type=F32)


def right_mul(x, tab):
    xh, xl = split(x)
    return dot(xh, tab[0]) + (dot(xl, tab[0]) + dot(xh, tab[1]))


def left_mul(tab, y):
    yh, yl = split(y)
    return dot(tab[0], yh) + (dot(tab[0], yl) + dot(tab[1], yh))


def pair(u0, u1):
    top = jnp.concatenate([u0[:, :W], u1[:, :W]], 1)
    return jnp.concatenate([top, jnp.concatenate([u0[:, W:], u1[:, W:]], 1)], 0)


def both(fields, rtab, ltab):
    x = jnp.concatenate([jnp.concatenate([r, i], 1) for r, i in fields], 0)
    y = right_mul(x, rtab)
    out = []
    for p in range(2):
        z = left_mul(ltab, pair(y[2 * p * W : (2 * p + 1) * W], y[(2 * p + 1) * W : (2 * p + 2) * W]))
        out.append((z[:W, :W], z[W:, :W]))
        out.append((z[:W, W:], z[W:, W:]))
    return out


def cmul(a, b):
    return a[0] * b[0] - a[1] * b[1], a[0] * b[1] + a[1] * b[0]


def cmulc(a, b):
    return a[0] * b[0] + a[1] * b[1], a[0] * b[1] - a[1] * b[0]


def add(a, b):
    return a[0] + b[0], a[1] + b[1]


def kernel(
    off, cnt, obj, probe_hbm, meas_hbm, tab_hbm, gobj, gprobe,
    probe, meas, tab, ext0, ext1, win, tbuf, gt, gwin, pad, gext0, gext1, glow, gright,
    acc, rcore, ra, rb, zb, res, lsem, ssem, rsem,
):
    ty, tx = lax.axis_index("ty"), lax.axis_index("tx")
    core, y, xh = lax.rem(ty, 2), lax.rem(lax.div(ty, 2), 4), lax.div(ty, 8)
    z, x = lax.div(tx, 2), xh * 2 + lax.rem(tx, 2)

    def at(core, y, x, z):
        return {"ty": lax.div(x, 2) * 8 + y * 2 + core, "tx": z * 2 + lax.rem(x, 2)}

    ext, gext = (ext0, ext1), (gext0, gext1)
    local = []
    for src, dst in (
        (obj.at[0], ext0.at[:, 0, 0:W, :]),
        (obj.at[1], ext1.at[:, 0, 0:W, :]),
        (probe_hbm, probe),
        (tab_hbm, tab),
        (meas_hbm, meas),
    ):
        local.append(pltpu.make_async_copy(src, dst, lsem.at[len(local)]))
        local[-1].start()

    left, right = {"ty": ty, "tx": lax.rem(tx + 15, 16)}, {"ty": ty, "tx": lax.rem(tx + 1, 16)}
    upper, lower = {"ty": lax.rem(ty + 15, 16), "tx": tx}, {"ty": lax.rem(ty + 1, 16), "tx": tx}
    peers = [at(1 - core, y, x, z), left, right, upper, lower]
    peers += [at(core, lax.rem(y + k, 4), x, z) for k in range(1, 4)]
    peers += [at(core, y, lax.rem(x + k, 4), z) for k in range(1, 4)]
    peers += [at(core, y, x, lax.rem(z + k, 8)) for k in range(1, 8)]
    barrier = pltpu.get_barrier_semaphore()
    for peer in peers:
        pl.semaphore_signal(barrier, inc=1, device_id=peer, device_id_type=pl.DeviceIdType.MESH)
    pl.semaphore_wait(barrier, len(peers))

    sent = []

    def remote(src, dst, device):
        i = len(sent)
        copy = pltpu.make_async_remote_copy(
            src_ref=src, dst_ref=dst, send_sem=ssem.at[i], recv_sem=rsem.at[i],
            device_id=device, device_id_type=pl.DeviceIdType.MESH,
        )
        sent.append(copy)
        return copy

    from_right = [remote(obj.at[s], ext[s].at[:, 1, 0:W, :], left) for s in range(2)]
    from_lower = [remote(obj.at[s], ext[s].at[:, 0, W : 2 * W, :], upper) for s in range(2)]
    from_corner = [remote(ext[s].at[:, 1, 0:W, :], ext[s].at[:, 1, W : 2 * W, :], upper) for s in range(2)]
    for s in range(2):
        from_right[s].start()

        @pl.when(ty > 0)
        def _():
            from_lower[s].start()

    for s in range(2):
        from_right[s].wait_recv()

        @pl.when(ty > 0)
        def _():
            from_corner[s].start()

    lane = lax.broadcasted_iota(jnp.int32, (W, W), 1)

    def halo_wait(s):
        local[s].wait()

        @pl.when(ty < 15)
        def _():
            from_lower[s].wait_recv()
            from_corner[s].wait_recv()

    def cut(slot, s):
        oy, ox = off[0, slot], off[1, slot]
        shift = lax.rem(W - ox, W)
        parts = []
        for c in range(2):
            first = pltpu.roll(ext[s][c, 0, pl.ds(oy, W), :], shift, 1)
            second = pltpu.roll(ext[s][c, 1, pl.ds(oy, W), :], shift, 1)
            parts.append(jnp.where(lane < W - ox, first, second))
            win[s, slot, c] = parts[c]
        return tuple(parts)

    def scatter(s):
        zero = jnp.zeros((W, W), F32)
        for c in range(2):
            for slot in range(SLOTS):
                oy, ox = off[0, slot], off[1, slot]
                g = pltpu.roll(gwin[s, slot, c], ox, 1)
                for half, mask in ((0, lane >= ox), (1, lane < ox)):
                    pad[half, W : 2 * W, :] = jnp.where(mask, g, zero)
                for half in range(2):
                    v = pad[half, pl.ds(W - oy, 2 * W), :]
                    if slot == 0:
                        gext[s][c, half] = v
                    else:
                        gext[s][c, half] += v

    for part in (0, 2):
        pad[:, part * W : (part + 1) * W, :] = jnp.zeros((2, W, W), F32)
    local[2].wait()
    local[3].wait()
    local[4].wait()
    a_r, a_l, f_r, f_l = (tab.at[i] for i in range(4))

    halo_wait(0)

    def first_layer(slot, _):
        w0 = cut(slot, 0)
        ts = both([cmul((probe[m, 0], probe[m, 1]), w0) for m in range(MODES)], a_r, a_l)
        for m in range(MODES):
            tbuf[slot, m, 0], tbuf[slot, m, 1] = ts[m]
        return 0

    lax.fori_loop(0, SLOTS, first_layer, 0)
    halo_wait(1)

    def second_layer(slot, _):
        w1 = cut(slot, 1)
        far = both([cmul((tbuf[slot, m, 0], tbuf[slot, m, 1]), w1) for m in range(MODES)], f_r, f_l)
        intensity = sum(r * r + i * i for r, i in far)
        live = jnp.where(slot < cnt[0, 0], 2.0, 0.0)
        d = (intensity - meas[slot]) * live
        gw = both([(r * d, i * d) for r, i in far], f_l, f_r)
        total = None
        for m in range(MODES):
            gt[slot, m, 0], gt[slot, m, 1] = cmulc(w1, gw[m])
            g = cmulc((tbuf[slot, m, 0], tbuf[slot, m, 1]), gw[m])
            total = g if total is None else add(total, g)
        gwin[1, slot, 0], gwin[1, slot, 1] = total
        return 0

    lax.fori_loop(0, SLOTS, second_layer, 0)

    to_lower = [remote(gext[s].at[:, :, W : 2 * W, :], glow.at[s], lower) for s in range(2)]
    to_right = [remote(gext[s].at[:, 1, 0:W, :], gright.at[s], right) for s in range(2)]

    def send_down(s):
        scatter(s)

        @pl.when(ty < 15)
        def _():
            to_lower[s].start()

    def send_right(s):
        @pl.when(ty > 0)
        def _():
            to_lower[s].wait_recv()
            for c in range(2):
                for half in range(2):
                    gext[s][c, half, 0:W, :] += glow[s, c, half]

        to_right[s].start()

    def finish(s):
        to_right[s].wait_recv()
        for c in range(2):
            gobj[s, c] = gext[s][c, 0, 0:W, :] + gright[s, c]

    send_down(1)

    def span(start, size):
        return pl.ds(pl.multiple_of(start, size), size)

    def axes(m):
        on_y = [at(core, lax.rem(y + k, 4), x, z) for k in range(4)]
        on_x = [at(core, y, lax.rem(x + k, 4), z) for k in range(4)]
        return (y, x, on_y, on_x) if m < 2 else (x, y, on_x, on_y)

    other = at(1 - core, y, x, z)
    mine = core * W
    by_core, by_a, by_b, by_z, out_b, out_a, out_core = ([] for _ in range(7))
    for m in range(MODES):
        a, b, on_a, on_b = axes(m)
        place = mine + a * 32 + b * 8
        by_core.append(remote(acc.at[m, span((1 - core) * W, W), :], rcore.at[m], other))
        by_a.append([remote(acc.at[m, span(mine + lax.rem(a + k, 4) * 32, 32), :], ra.at[m, k - 1], on_a[k]) for k in range(1, 4)])
        by_b.append([remote(acc.at[m, span(mine + a * 32 + lax.rem(b + k, 4) * 8, 8), :], rb.at[m, k - 1], on_b[k]) for k in range(1, 4)])
        by_z.append([remote(zb.at[m, z], zb.at[m, z], at(core, y, x, lax.rem(z + k, 8))) for k in range(1, 8)])
        own = res.at[m, span(place, 8), :]
        out_b.append([remote(own, own, on_b[k]) for k in range(1, 4)])
        own = res.at[m, span(mine + a * 32, 32), :]
        out_a.append([remote(own, own, on_a[k]) for k in range(1, 4)])
        own = res.at[m, span(mine, W), :]
        out_core.append(remote(own, own, other))

    def start(copies):
        for copy in copies:
            copy.start()

    def arrive(copies):
        for copy in copies:
            copy.wait_recv()

    for m in range(MODES):
        p = (probe[m, 0], probe[m, 1])
        gu = both([(gt[s, m, 0], gt[s, m, 1]) for s in range(SLOTS)], a_l, a_r)
        total = None
        for s in range(SLOTS):
            g = cmulc(p, gu[s])
            for c in range(2):
                if m == 0:
                    gwin[0, s, c] = g[c]
                else:
                    gwin[0, s, c] += g[c]
            q = cmulc((win[0, s, 0], win[0, s, 1]), gu[s])
            total = q if total is None else add(total, q)
        acc[m, 0:W, :], acc[m, W : 2 * W, :] = total
        by_core[m].start()

    send_right(1)
    for m in range(MODES):
        by_core[m].wait_recv()
        acc[m, span(mine, W), :] += rcore[m]
        start(by_a[m])
    send_down(0)
    for m in range(MODES):
        a, _, _, _ = axes(m)
        arrive(by_a[m])
        acc[m, span(mine + a * 32, 32), :] += ra[m, 0] + ra[m, 1] + ra[m, 2]
        start(by_b[m])
    finish(1)
    for m in range(MODES):
        a, b, _, _ = axes(m)
        arrive(by_b[m])
        zb[m, z] = acc[m, span(mine + a * 32 + b * 8, 8), :] + (rb[m, 0] + rb[m, 1] + rb[m, 2])
        start(by_z[m])
    send_right(0)
    for m in range(MODES):
        a, b, _, _ = axes(m)
        arrive(by_z[m])
        total = zb[m, 0]
        for k in range(1, 8):
            total = total + zb[m, k]
        res[m, span(mine + a * 32 + b * 8, 8), :] = total
        start(out_b[m])
    for m in range(MODES):
        arrive(out_b[m])
        start(out_a[m])
    finish(0)
    for m in range(MODES):
        arrive(out_a[m])
        out_core[m].start()
    for m in range(MODES):
        out_core[m].wait_recv()
        gprobe[m, 0] = res[m, 0:W, :]
        gprobe[m, 1] = res[m, W : 2 * W, :]

    up, down = from_lower + from_corner, to_lower
    for copy in sent:
        if not any(copy is c for c in up + down):
            copy.wait_send()

    @pl.when(ty > 0)
    def _():
        for copy in up:
            copy.wait_send()

    @pl.when(ty < 15)
    def _():
        for copy in down:
            copy.wait_send()


COPIES = 10 + MODES * 21


def on_device(object_slices, probe, measured, offsets, counts):
    smem, vmem, hbm = (pl.BlockSpec(memory_space=s) for s in (pltpu.SMEM, pltpu.VMEM, pl.ANY))
    shapes = [
        (MODES, 2, W, W),
        (SLOTS, W, W),
        None,
        (2, 2, 2 * W, W),
        (2, 2, 2 * W, W),
        (2, SLOTS, 2, W, W),
        (SLOTS, MODES, 2, W, W),
        (SLOTS, MODES, 2, W, W),
        (2, SLOTS, 2, W, W),
        (2, 3 * W, W),
        (2, 2, 2 * W, W),
        (2, 2, 2 * W, W),
        (2, 2, 2, W, W),
        (2, 2, W, W),
        (MODES, 2 * W, W),
        (MODES, W, W),
        (MODES, 3, 32, W),
        (MODES, 3, 8, W),
        (MODES, 8, 8, W),
        (MODES, 2 * W, W),
    ]
    scratch = [pltpu.VMEM(s, F32) if s else pltpu.VMEM((4, 2, 2 * W, 2 * W), BF16) for s in shapes]
    scratch += [pltpu.SemaphoreType.DMA((5,)), pltpu.SemaphoreType.DMA((COPIES,)), pltpu.SemaphoreType.DMA((COPIES,))]
    return pl.pallas_call(
        kernel,
        out_shape=(jax.ShapeDtypeStruct((2, 2, W, W), F32), jax.ShapeDtypeStruct((MODES, 2, W, W), F32)),
        in_specs=[smem, smem, hbm, hbm, hbm, hbm],
        out_specs=(vmem, vmem),
        scratch_shapes=scratch,
        compiler_params=pltpu.CompilerParams(collective_id=0, has_side_effects=True),
    )(
        offsets.reshape(2, SLOTS), counts, object_slices, probe, measured.reshape(SLOTS, W, W), jnp.asarray(tables())
    )


def solution(mesh):
    in_specs = (
        P(None, None, "ty", "tx"),
        P(),
        P("ty", "tx", None, None, None),
        P(None, "ty", "tx", None),
        P("ty", "tx"),
    )
    out_specs = (P(None, None, "ty", "tx"), P())
    return jax.shard_map(
        on_device, mesh=mesh, in_specs=in_specs, out_specs=out_specs, check_vma=False
    )
```

profile of v0, /device:TPU:1, one launch (start us, length us, event | category | flops | bytes accessed | tf_op | source)
XLA Modules:
  0.0 72.4 jit_solution(9279689105055284470)
XLA Ops:
  1.3 68.6 %shard_map.77 = (f32[2,2,128,128]{3,2,1,0:T(8,128)}, f32[4,2,128,128]{3,2,1,0:T(8,128)}) custom-call(s32[2,4]{1,0:T(2,128)} %bitcast.3, s32[1,1]{1,0:T(1,128)S(6)} %copy.10.cnt, f32[2,2,128,128]{3,2,1,0:T(8,128)} %obj.1, f32[4,2,128,128]{3,2,1,0:T(8,128)} %probe_hbm.1, f32[4,128,128]{2,1,0:T(8,128)} %bitcast.2, bf16[4,2,256,256]{3,2,1,0:T(8,128)(2,1)} %constant.2.clone.tab_hbm), custom_call_target="tpu_custom_call" | custom-call | tf_op jit(solution)/shard_map/pallas_call | solution.py:375
  69.9 0.0 copy-start
  69.9 1.7 %copy.11 = f32[2,2,128,128]{3,2,1,0:T(8,128)} copy(f32[2,2,128,128]{3,2,1,0:T(8,128)} %get-tuple-element.4) | data formatting | bytes 524288
  71.6 0.0 copy-done
  71.6 0.8 %copy.12 = f32[4,2,128,128]{3,2,1,0:T(8,128)} copy(f32[4,2,128,128]{3,2,1,0:T(8,128)S(1)} %copy-done) | data formatting | bytes 1048576
Async XLA Ops:
  69.9 1.7 %copy-start = (f32[4,2,128,128]{3,2,1,0:T(8,128)S(1)}, f32[4,2,128,128]{3,2,1,0:T(8,128)}, u32[]{:S(2)}) copy-start(f32[4,2,128,128]{3,2,1,0:T(8,128)} %get-tuple-element.5) | copy-start | bytes 1572868
where the time goes:
time: 72.6 us; the launch traced here: 72.4 us
  Pallas kernels  68.6 us (94%)
  local copies, waits for them, and re-layouts  2.52 us (3%)
  between operations  1.29 us (2%)
    pallas_call x1, Pallas kernels, on_device(): pl.pallas_call(kernel, out_shape=(jax.ShapeDtypeStruct((2, 2, W, W), F32)...  68.6 us
    unnamed x4, local copies, waits for them, and re-layouts  2.52 us

commit v1 on v0

--- a/solution.py
+++ b/solution.py
@@ -80,8 +80,8 @@
 
 def kernel(
     off, cnt, obj, probe_hbm, meas_hbm, tab_hbm, gobj, gprobe,
-    probe, meas, tab, ext0, ext1, win, tbuf, gt, gwin, pad, gext0, gext1, glow, gright,
-    acc, rcore, ra, rb, zb, res, lsem, ssem, rsem,
+    probe, meas, tab, ext0, ext1, win, tbuf, gt, gwin, pad, gext0, gext1, glow, gright, gside, gfar,
+    acc, rcore, rp, zb, res, lsem, ssem, rsem,
 ):
     ty, tx = lax.axis_index("ty"), lax.axis_index("tx")
     core, y, xh = lax.rem(ty, 2), lax.rem(lax.div(ty, 2), 4), lax.div(ty, 8)
@@ -105,9 +105,11 @@
     left, right = {"ty": ty, "tx": lax.rem(tx + 15, 16)}, {"ty": ty, "tx": lax.rem(tx + 1, 16)}
     upper, lower = {"ty": lax.rem(ty + 15, 16), "tx": tx}, {"ty": lax.rem(ty + 1, 16), "tx": tx}
     peers = [at(1 - core, y, x, z), left, right, upper, lower]
-    peers += [at(core, lax.rem(y + k, 4), x, z) for k in range(1, 4)]
-    peers += [at(core, y, lax.rem(x + k, 4), z) for k in range(1, 4)]
-    peers += [at(core, y, x, lax.rem(z + k, 8)) for k in range(1, 8)]
+    peers += [{"ty": lax.rem(ty + 15, 16), "tx": lax.rem(tx + 15, 16)}, {"ty": lax.rem(ty + 1, 16), "tx": lax.rem(tx + 1, 16)}]
+    plane = [(j, i) for j in (2, 1, 3, 0) for i in (2, 1, 3, 0)][:-1]
+    in_plane = [at(core, lax.rem(y + j, 4), lax.rem(x + i, 4), z) for j, i in plane]
+    in_line = [at(core, y, x, lax.rem(z + k, 8)) for k in (4, 3, 5, 2, 6, 1, 7)]
+    peers += in_plane + in_line
     barrier = pltpu.get_barrier_semaphore()
     for peer in peers:
         pl.semaphore_signal(barrier, inc=1, device_id=peer, device_id_type=pl.DeviceIdType.MESH)
@@ -124,32 +126,79 @@
         sent.append(copy)
         return copy
 
-    from_right = [remote(obj.at[s], ext[s].at[:, 1, 0:W, :], left) for s in range(2)]
-    from_lower = [remote(obj.at[s], ext[s].at[:, 0, W : 2 * W, :], upper) for s in range(2)]
-    from_corner = [remote(ext[s].at[:, 1, 0:W, :], ext[s].at[:, 1, W : 2 * W, :], upper) for s in range(2)]
+    from_right, from_lower, from_corner, far_corner, far_lower, far_direct = ([] for _ in range(6))
+    up_left = {"ty": lax.rem(ty + 15, 16), "tx": lax.rem(tx + 15, 16)}
     for s in range(2):
-        from_right[s].start()
-
-        @pl.when(ty > 0)
+        from_right.append([remote(obj.at[s, c], ext[s].at[c, 1, 0:W, :], left) for c in range(2)])
+        from_lower.append(remote(obj.at[s], ext[s].at[:, 0, W : 2 * W, :], upper))
+        from_corner.append([remote(ext[s].at[c, 1, 0:W, :], ext[s].at[c, 1, W : 2 * W, :], upper) for c in range(2)])
+        far_corner.append([remote(obj.at[s, c], ext[s].at[c, 1, W : 2 * W, :], up_left) for c in range(2)])
+        far_lower.append(remote(ext[s].at[0, 1, W : 2 * W, :], ext[s].at[0, 0, W : 2 * W, :], right))
+        far_direct.append(remote(obj.at[s, 1], ext[s].at[1, 0, W : 2 * W, :], upper))
+    sends_up = jnp.logical_and(ty > 0, ty != 8)
+    gets_up = jnp.logical_and(ty < 15, ty != 7)
+    first = tx == 0
+    sends_far, gets_far = jnp.logical_and(ty == 8, tx > 0), jnp.logical_and(ty == 7, tx < 15)
+    sends_direct, gets_direct = jnp.logical_and(ty == 8, first), jnp.logical_and(ty == 7, first)
+    gets_relayed = jnp.logical_and(ty == 7, tx > 0)
+
+    def send_left(s):
+        for copy in from_right[s]:
+            copy.start()
+
+    def send_up(s):
+        @pl.when(jnp.logical_or(sends_up, sends_direct))
         def _():
             from_lower[s].start()
 
-    for s in range(2):
-        from_right[s].wait_recv()
-
-        @pl.when(ty > 0)
-        def _():
-            from_corner[s].start()
+    def relay(s):
+        @pl.when(gets_far)
+        def _():
+            far_corner[s][0].wait_recv()
+            far_lower[s].start()
+
+        for c in range(2):
+            from_right[s][c].wait_recv()
+
+            @pl.when(sends_up)
+            def _():
+                from_corner[s][c].start()
+
+    def send_far_up(s):
+        @pl.when(sends_far)
+        def _():
+            for copy in (*far_corner[s], far_direct[s]):
+                copy.start()
+
+    send_far_up(0)
+    send_up(0)
+    send_left(0)
+    relay(0)
+    send_far_up(1)
+    send_left(1)
 
     lane = lax.broadcasted_iota(jnp.int32, (W, W), 1)
 
     def halo_wait(s):
         local[s].wait()
 
-        @pl.when(ty < 15)
+        @pl.when(jnp.logical_or(gets_up, gets_direct))
         def _():
             from_lower[s].wait_recv()
-            from_corner[s].wait_recv()
+
+        @pl.when(gets_up)
+        def _():
+            for copy in from_corner[s]:
+                copy.wait_recv()
+
+        @pl.when(gets_relayed)
+        def _():
+            far_lower[s].wait_recv()
+            far_direct[s].wait_recv()
+
+        @pl.when(gets_far)
+        def _():
+            far_corner[s][1].wait_recv()
 
     def cut(slot, s):
         oy, ox = off[0, slot], off[1, slot]
@@ -185,6 +234,7 @@
     a_r, a_l, f_r, f_l = (tab.at[i] for i in range(4))
 
     halo_wait(0)
+    send_up(1)
 
     def first_layer(slot, _):
         w0 = cut(slot, 0)
@@ -193,7 +243,9 @@
             tbuf[slot, m, 0], tbuf[slot, m, 1] = ts[m]
         return 0
 
-    lax.fori_loop(0, SLOTS, first_layer, 0)
+    lax.fori_loop(0, SLOTS // 2, first_layer, 0)
+    relay(1)
+    lax.fori_loop(SLOTS // 2, SLOTS, first_layer, 0)
     halo_wait(1)
 
     def second_layer(slot, _):
@@ -215,16 +267,31 @@
 
     to_lower = [remote(gext[s].at[:, :, W : 2 * W, :], glow.at[s], lower) for s in range(2)]
     to_right = [remote(gext[s].at[:, 1, 0:W, :], gright.at[s], right) for s in range(2)]
+    side = [remote(gext[s].at[:, 1, W : 2 * W, :], gside.at[s], right) for s in range(2)]
+    down_far = [remote(gext[s].at[:, 0, W : 2 * W, :], gfar.at[s], lower) for s in range(2)]
 
     def send_down(s):
         scatter(s)
 
-        @pl.when(ty < 15)
+        @pl.when(ty == 7)
+        def _():
+            side[s].start()
+
+    def down(s):
+        @pl.when(gets_up)
         def _():
             to_lower[s].start()
 
+    def send_far(s):
+        @pl.when(ty == 7)
+        def _():
+            side[s].wait_recv()
+            for c in range(2):
+                gext[s][c, 0, W : 2 * W, :] += gside[s, c]
+            down_far[s].start()
+
     def send_right(s):
-        @pl.when(ty > 0)
+        @pl.when(sends_up)
         def _():
             to_lower[s].wait_recv()
             for c in range(2):
@@ -234,36 +301,42 @@
         to_right[s].start()
 
     def finish(s):
+        @pl.when(ty == 8)
+        def _():
+            down_far[s].wait_recv()
+            for c in range(2):
+                gext[s][c, 0, 0:W, :] += gfar[s, c]
+
         to_right[s].wait_recv()
         for c in range(2):
             gobj[s, c] = gext[s][c, 0, 0:W, :] + gright[s, c]
 
     send_down(1)
+    down(1)
 
     def span(start, size):
         return pl.ds(pl.multiple_of(start, size), size)
 
-    def axes(m):
-        on_y = [at(core, lax.rem(y + k, 4), x, z) for k in range(4)]
-        on_x = [at(core, y, lax.rem(x + k, 4), z) for k in range(4)]
-        return (y, x, on_y, on_x) if m < 2 else (x, y, on_x, on_y)
-
     other = at(1 - core, y, x, z)
     mine = core * W
-    by_core, by_a, by_b, by_z, out_b, out_a, out_core = ([] for _ in range(7))
+    place = span(mine + (y * 4 + x) * 8, 8)
+    by_core, by_plane = [], []
     for m in range(MODES):
-        a, b, on_a, on_b = axes(m)
-        place = mine + a * 32 + b * 8
         by_core.append(remote(acc.at[m, span((1 - core) * W, W), :], rcore.at[m], other))
-        by_a.append([remote(acc.at[m, span(mine + lax.rem(a + k, 4) * 32, 32), :], ra.at[m, k - 1], on_a[k]) for k in range(1, 4)])
-        by_b.append([remote(acc.at[m, span(mine + a * 32 + lax.rem(b + k, 4) * 8, 8), :], rb.at[m, k - 1], on_b[k]) for k in range(1, 4)])
-        by_z.append([remote(zb.at[m, z], zb.at[m, z], at(core, y, x, lax.rem(z + k, 8))) for k in range(1, 8)])
-        own = res.at[m, span(place, 8), :]
-        out_b.append([remote(own, own, on_b[k]) for k in range(1, 4)])
-        own = res.at[m, span(mine + a * 32, 32), :]
-        out_a.append([remote(own, own, on_a[k]) for k in range(1, 4)])
-        own = res.at[m, span(mine, W), :]
-        out_core.append(remote(own, own, other))
+        by_plane.append([
+            remote(acc.at[m, span(mine + (lax.rem(y + j, 4) * 4 + lax.rem(x + i, 4)) * 8, 8), :], rp.at[m, k], in_plane[k])
+            for k, (j, i) in enumerate(plane)
+        ])
+    by_line, out_plane, out_core = [], [], []
+    for g in range(2):
+        pair_of = pl.ds(2 * g, 2)
+        by_line.append([remote(zb.at[g, z], zb.at[g, z], device) for device in in_line])
+        own = res.at[pair_of, place, :]
+        out_plane.append([remote(own, own, device) for device in in_plane])
+        out_core.append([])
+        for j in (0, 1, 3, 2):
+            own = res.at[pair_of, span(mine + lax.rem(y + 4 - j, 4) * 32, 32), :]
+            out_core[g].append((j, remote(own, own, other)))
 
     def start(copies):
         for copy in copies:
@@ -272,6 +345,11 @@
     def arrive(copies):
         for copy in copies:
             copy.wait_recv()
+
+    def scatter_core(m):
+        by_core[m].wait_recv()
+        acc[m, span(mine, W), :] += rcore[m]
+        start(by_plane[m])
 
     for m in range(MODES):
         p = (probe[m, 0], probe[m, 1])
@@ -288,62 +366,68 @@
             total = q if total is None else add(total, q)
         acc[m, 0:W, :], acc[m, W : 2 * W, :] = total
         by_core[m].start()
-
+        if m > 0:
+            scatter_core(m - 1)
+        if m == MODES - 1:
+            send_far(1)
+
+    scatter_core(MODES - 1)
+    send_down(0)
+    down(0)
     send_right(1)
-    for m in range(MODES):
-        by_core[m].wait_recv()
-        acc[m, span(mine, W), :] += rcore[m]
-        start(by_a[m])
-    send_down(0)
-    for m in range(MODES):
-        a, _, _, _ = axes(m)
-        arrive(by_a[m])
-        acc[m, span(mine + a * 32, 32), :] += ra[m, 0] + ra[m, 1] + ra[m, 2]
-        start(by_b[m])
+    for g in range(2):
+        for i in range(2):
+            m = 2 * g + i
+            arrive(by_plane[m])
+            total = acc[m, place, :]
+            for k in range(15):
+                total = total + rp[m, k]
+            zb[g, z, i] = total
+        start(by_line[g])
+    send_far(0)
+    send_right(0)
+    for g in range(2):
+        arrive(by_line[g])
+        for i in range(2):
+            total = zb[g, 0, i]
+            for k in range(1, 8):
+                total = total + zb[g, k, i]
+            res[2 * g + i, place, :] = total
+        start(out_plane[g])
+    for g in range(2):
+        for j, copy in out_core[g]:
+            arrive([out_plane[g][k] for k in range(15) if plane[k][0] == j])
+            copy.start()
     finish(1)
-    for m in range(MODES):
-        a, b, _, _ = axes(m)
-        arrive(by_b[m])
-        zb[m, z] = acc[m, span(mine + a * 32 + b * 8, 8), :] + (rb[m, 0] + rb[m, 1] + rb[m, 2])
-        start(by_z[m])
-    send_right(0)
-    for m in range(MODES):
-        a, b, _, _ = axes(m)
-        arrive(by_z[m])
-        total = zb[m, 0]
-        for k in range(1, 8):
-            total = total + zb[m, k]
-        res[m, span(mine + a * 32 + b * 8, 8), :] = total
-        start(out_b[m])
-    for m in range(MODES):
-        arrive(out_b[m])
-        start(out_a[m])
     finish(0)
-    for m in range(MODES):
-        arrive(out_a[m])
-        out_core[m].start()
-    for m in range(MODES):
-        out_core[m].wait_recv()
-        gprobe[m, 0] = res[m, 0:W, :]
-        gprobe[m, 1] = res[m, W : 2 * W, :]
-
-    up, down = from_lower + from_corner, to_lower
+    for g in range(2):
+        for _, copy in out_core[g]:
+            copy.wait_recv()
+        for m in (2 * g, 2 * g + 1):
+            gprobe[m, 0] = res[m, 0:W, :]
+            gprobe[m, 1] = res[m, W : 2 * W, :]
+
+    groups = (
+        (jnp.logical_or(sends_up, sends_direct), from_lower),
+        (sends_up, from_corner[0] + from_corner[1]),
+        (sends_far, far_corner[0] + far_corner[1] + far_direct),
+        (gets_far, far_lower),
+        (gets_up, to_lower),
+        (ty == 7, side + down_far),
+    )
+    some = [id(copy) for _, copies in groups for copy in copies]
     for copy in sent:
-        if not any(copy is c for c in up + down):
+        if id(copy) not in some:
             copy.wait_send()
-
-    @pl.when(ty > 0)
-    def _():
-        for copy in up:
-            copy.wait_send()
-
-    @pl.when(ty < 15)
-    def _():
-        for copy in down:
-            copy.wait_send()
-
-
-COPIES = 10 + MODES * 21
+    for condition, copies in groups:
+
+        @pl.when(condition)
+        def _():
+            for copy in copies:
+                copy.wait_send()
+
+
+COPIES = 26 + MODES * 16 + 2 * 26
 
 
 def on_device(object_slices, probe, measured, offsets, counts):
@@ -363,11 +447,12 @@
         (2, 2, 2 * W, W),
         (2, 2, 2, W, W),
         (2, 2, W, W),
+        (2, 2, W, W),
+        (2, 2, W, W),
         (MODES, 2 * W, W),
         (MODES, W, W),
-        (MODES, 3, 32, W),
-        (MODES, 3, 8, W),
-        (MODES, 8, 8, W),
+        (MODES, 15, 8, W),
+        (2, 8, 2, 8, W),
         (MODES, 2 * W, W),
     ]
     scratch = [pltpu.VMEM(s, F32) if s else pltpu.VMEM((4, 2, 2 * W, 2 * W), BF16) for s in shapes]

time: 72.6 us -> 65.7 us (0.905)
  Pallas kernels: 68.6 us -> 61.8 us
    pallas_call x1, Pallas kernels: 68.6 us -> 61.8 us  [on_device(): pl.pallas_call(kernel, out_shape=(jax.ShapeDtypeStruct((2, 2, W, W), F32)...]
where the time goes in v1:
time: 65.7 us; the launch traced here: 65.6 us
  Pallas kernels  61.8 us (94%)
  local copies, waits for them, and re-layouts  2.52 us (4%)
  between operations  1.29 us (2%)
    pallas_call x1, Pallas kernels, on_device(): pl.pallas_call(kernel, out_shape=(jax.ShapeDtypeStruct((2, 2, W, W), F32)...  61.8 us
    unnamed x4, local copies, waits for them, and re-layouts  2.52 us

profile of v1, /device:TPU:1, one launch (start us, length us, event | category | flops | bytes accessed | tf_op | source)
XLA Modules:
  0.0 65.6 jit_solution(8238890208850464580)
XLA Ops:
  1.3 61.8 %shard_map.77 = (f32[2,2,128,128]{3,2,1,0:T(8,128)}, f32[4,2,128,128]{3,2,1,0:T(8,128)}) custom-call(s32[2,4]{1,0:T(2,128)} %bitcast.3, s32[1,1]{1,0:T(1,128)S(6)} %copy.10.cnt, f32[2,2,128,128]{3,2,1,0:T(8,128)} %obj.1, f32[4,2,128,128]{3,2,1,0:T(8,128)} %probe_hbm.1, f32[4,128,128]{2,1,0:T(8,128)} %bitcast.2, bf16[4,2,256,256]{3,2,1,0:T(8,128)(2,1)} %constant.2.clone.tab_hbm), custom_call_target="tpu_custom_call" | custom-call | tf_op jit(solution)/shard_map/pallas_call | solution.py:460
  63.0 0.0 copy-start
  63.1 1.7 %copy.11 = f32[2,2,128,128]{3,2,1,0:T(8,128)} copy(f32[2,2,128,128]{3,2,1,0:T(8,128)} %get-tuple-element.4) | data formatting | bytes 524288
  64.8 0.0 copy-done
  64.8 0.8 %copy.12 = f32[4,2,128,128]{3,2,1,0:T(8,128)} copy(f32[4,2,128,128]{3,2,1,0:T(8,128)S(1)} %copy-done) | data formatting | bytes 1048576
Async XLA Ops:
  63.0 1.7 %copy-start = (f32[4,2,128,128]{3,2,1,0:T(8,128)S(1)}, f32[4,2,128,128]{3,2,1,0:T(8,128)}, u32[]{:S(2)}) copy-start(f32[4,2,128,128]{3,2,1,0:T(8,128)} %get-tuple-element.5) | copy-start | bytes 1572868

commit v2 on v1

--- a/solution.py
+++ b/solution.py
@@ -56,11 +56,11 @@
 
 
 def both(fields, rtab, ltab):
-    x = jnp.concatenate([jnp.concatenate([r, i], 1) for r, i in fields], 0)
-    y = right_mul(x, rtab)
     out = []
-    for p in range(2):
-        z = left_mul(ltab, pair(y[2 * p * W : (2 * p + 1) * W], y[(2 * p + 1) * W : (2 * p + 2) * W]))
+    for p in range(0, len(fields), 2):
+        x = jnp.concatenate([jnp.concatenate([r, i], 1) for r, i in fields[p : p + 2]], 0)
+        y = right_mul(x, rtab)
+        z = left_mul(ltab, pair(y[:W], y[W:]))
         out.append((z[:W, :W], z[W:, :W]))
         out.append((z[:W, W:], z[W:, W:]))
     return out
@@ -126,15 +126,15 @@
         sent.append(copy)
         return copy
 
-    from_right, from_lower, from_corner, far_corner, far_lower, far_direct = ([] for _ in range(6))
+    from_right, from_lower, from_corner, far_corner = ([] for _ in range(4))
     up_left = {"ty": lax.rem(ty + 15, 16), "tx": lax.rem(tx + 15, 16)}
     for s in range(2):
         from_right.append([remote(obj.at[s, c], ext[s].at[c, 1, 0:W, :], left) for c in range(2)])
         from_lower.append(remote(obj.at[s], ext[s].at[:, 0, W : 2 * W, :], upper))
         from_corner.append([remote(ext[s].at[c, 1, 0:W, :], ext[s].at[c, 1, W : 2 * W, :], upper) for c in range(2)])
         far_corner.append([remote(obj.at[s, c], ext[s].at[c, 1, W : 2 * W, :], up_left) for c in range(2)])
-        far_lower.append(remote(ext[s].at[0, 1, W : 2 * W, :], ext[s].at[0, 0, W : 2 * W, :], right))
-        far_direct.append(remote(obj.at[s, 1], ext[s].at[1, 0, W : 2 * W, :], upper))
+    far_lower = remote(ext0.at[0, 1, W : 2 * W, :], ext0.at[0, 0, W : 2 * W, :], right)
+    far_direct = remote(obj.at[0, 1], ext0.at[1, 0, W : 2 * W, :], upper)
     sends_up = jnp.logical_and(ty > 0, ty != 8)
     gets_up = jnp.logical_and(ty < 15, ty != 7)
     first = tx == 0
@@ -147,15 +147,17 @@
             copy.start()
 
     def send_up(s):
-        @pl.when(jnp.logical_or(sends_up, sends_direct))
+        @pl.when(jnp.logical_or(sends_up, sends_direct) if s == 0 else ty > 0)
         def _():
             from_lower[s].start()
 
     def relay(s):
-        @pl.when(gets_far)
-        def _():
-            far_corner[s][0].wait_recv()
-            far_lower[s].start()
+        if s == 0:
+
+            @pl.when(gets_far)
+            def _():
+                far_corner[0][0].wait_recv()
+                far_lower.start()
 
         for c in range(2):
             from_right[s][c].wait_recv()
@@ -167,22 +169,23 @@
     def send_far_up(s):
         @pl.when(sends_far)
         def _():
-            for copy in (*far_corner[s], far_direct[s]):
+            for copy in (*far_corner[s], *([far_direct] if s == 0 else [])):
                 copy.start()
 
     send_far_up(0)
     send_up(0)
     send_left(0)
+    send_left(1)
     relay(0)
     send_far_up(1)
-    send_left(1)
+    send_up(1)
 
     lane = lax.broadcasted_iota(jnp.int32, (W, W), 1)
 
     def halo_wait(s):
         local[s].wait()
 
-        @pl.when(jnp.logical_or(gets_up, gets_direct))
+        @pl.when(jnp.logical_or(gets_up, gets_direct) if s == 0 else ty < 15)
         def _():
             from_lower[s].wait_recv()
 
@@ -193,12 +196,14 @@
 
         @pl.when(gets_relayed)
         def _():
-            far_lower[s].wait_recv()
-            far_direct[s].wait_recv()
+            if s == 0:
+                far_lower.wait_recv()
+                far_direct.wait_recv()
 
         @pl.when(gets_far)
         def _():
-            far_corner[s][1].wait_recv()
+            for copy in far_corner[s][1 - s :]:
+                copy.wait_recv()
 
     def cut(slot, s):
         oy, ox = off[0, slot], off[1, slot]
@@ -234,21 +239,21 @@
     a_r, a_l, f_r, f_l = (tab.at[i] for i in range(4))
 
     halo_wait(0)
-    send_up(1)
-
-    def first_layer(slot, _):
+
+    def first_layer(slot):
         w0 = cut(slot, 0)
         ts = both([cmul((probe[m, 0], probe[m, 1]), w0) for m in range(MODES)], a_r, a_l)
         for m in range(MODES):
             tbuf[slot, m, 0], tbuf[slot, m, 1] = ts[m]
-        return 0
-
-    lax.fori_loop(0, SLOTS // 2, first_layer, 0)
+
+    for slot in range(0, SLOTS // 2):
+        first_layer(slot)
     relay(1)
-    lax.fori_loop(SLOTS // 2, SLOTS, first_layer, 0)
+    for slot in range(SLOTS // 2, SLOTS):
+        first_layer(slot)
     halo_wait(1)
 
-    def second_layer(slot, _):
+    def second_layer(slot):
         w1 = cut(slot, 1)
         far = both([cmul((tbuf[slot, m, 0], tbuf[slot, m, 1]), w1) for m in range(MODES)], f_r, f_l)
         intensity = sum(r * r + i * i for r, i in far)
@@ -261,9 +266,9 @@
             g = cmulc((tbuf[slot, m, 0], tbuf[slot, m, 1]), gw[m])
             total = g if total is None else add(total, g)
         gwin[1, slot, 0], gwin[1, slot, 1] = total
-        return 0
-
-    lax.fori_loop(0, SLOTS, second_layer, 0)
+
+    for slot in range(SLOTS):
+        second_layer(slot)
 
     to_lower = [remote(gext[s].at[:, :, W : 2 * W, :], glow.at[s], lower) for s in range(2)]
     to_right = [remote(gext[s].at[:, 1, 0:W, :], gright.at[s], right) for s in range(2)]
@@ -320,13 +325,11 @@
     other = at(1 - core, y, x, z)
     mine = core * W
     place = span(mine + (y * 4 + x) * 8, 8)
-    by_core, by_plane = [], []
-    for m in range(MODES):
-        by_core.append(remote(acc.at[m, span((1 - core) * W, W), :], rcore.at[m], other))
-        by_plane.append([
-            remote(acc.at[m, span(mine + (lax.rem(y + j, 4) * 4 + lax.rem(x + i, 4)) * 8, 8), :], rp.at[m, k], in_plane[k])
-            for k, (j, i) in enumerate(plane)
-        ])
+    by_core = [remote(acc.at[m, span((1 - core) * W, W), :], rcore.at[m], other) for m in range(MODES)]
+    by_plane = []
+    for g in range(2):
+        spots = [span(mine + (lax.rem(y + j, 4) * 4 + lax.rem(x + i, 4)) * 8, 8) for j, i in plane]
+        by_plane.append([remote(acc.at[pl.ds(2 * g, 2), spots[k], :], rp.at[g, k], in_plane[k]) for k in range(15)])
     by_line, out_plane, out_core = [], [], []
     for g in range(2):
         pair_of = pl.ds(2 * g, 2)
@@ -346,10 +349,11 @@
         for copy in copies:
             copy.wait_recv()
 
-    def scatter_core(m):
-        by_core[m].wait_recv()
-        acc[m, span(mine, W), :] += rcore[m]
-        start(by_plane[m])
+    def scatter_core(g):
+        for m in (2 * g, 2 * g + 1):
+            by_core[m].wait_recv()
+            acc[m, span(mine, W), :] += rcore[m]
+        start(by_plane[g])
 
     for m in range(MODES):
         p = (probe[m, 0], probe[m, 1])
@@ -365,27 +369,28 @@
             q = cmulc((win[0, s, 0], win[0, s, 1]), gu[s])
             total = q if total is None else add(total, q)
         acc[m, 0:W, :], acc[m, W : 2 * W, :] = total
-        by_core[m].start()
-        if m > 0:
-            scatter_core(m - 1)
+        if m % 2 == 0:
+            continue
+        start(by_core[m - 1 : m + 1])
         if m == MODES - 1:
             send_far(1)
-
-    scatter_core(MODES - 1)
+            scatter_core(0)
+
+    scatter_core(1)
     send_down(0)
-    down(0)
-    send_right(1)
     for g in range(2):
         for i in range(2):
             m = 2 * g + i
-            arrive(by_plane[m])
+            if i == 0:
+                arrive(by_plane[g])
             total = acc[m, place, :]
             for k in range(15):
-                total = total + rp[m, k]
+                total = total + rp[g, k, i]
             zb[g, z, i] = total
         start(by_line[g])
+    send_right(1)
+    down(0)
     send_far(0)
-    send_right(0)
     for g in range(2):
         arrive(by_line[g])
         for i in range(2):
@@ -394,6 +399,7 @@
                 total = total + zb[g, k, i]
             res[2 * g + i, place, :] = total
         start(out_plane[g])
+    send_right(0)
     for g in range(2):
         for j, copy in out_core[g]:
             arrive([out_plane[g][k] for k in range(15) if plane[k][0] == j])
@@ -408,10 +414,11 @@
             gprobe[m, 1] = res[m, W : 2 * W, :]
 
     groups = (
-        (jnp.logical_or(sends_up, sends_direct), from_lower),
+        (jnp.logical_or(sends_up, sends_direct), from_lower[:1]),
+        (ty > 0, from_lower[1:]),
         (sends_up, from_corner[0] + from_corner[1]),
-        (sends_far, far_corner[0] + far_corner[1] + far_direct),
-        (gets_far, far_lower),
+        (sends_far, far_corner[0] + far_corner[1] + [far_direct]),
+        (gets_far, [far_lower]),
         (gets_up, to_lower),
         (ty == 7, side + down_far),
     )
@@ -427,7 +434,7 @@
                 copy.wait_send()
 
 
-COPIES = 26 + MODES * 16 + 2 * 26
+COPIES = 24 + MODES + 2 * 41
 
 
 def on_device(object_slices, probe, measured, offsets, counts):
@@ -451,7 +458,7 @@
         (2, 2, W, W),
         (MODES, 2 * W, W),
         (MODES, W, W),
-        (MODES, 15, 8, W),
+        (2, 15, 2, 8, W),
         (2, 8, 2, 8, W),
         (MODES, 2 * W, W),
     ]

time: 65.7 us -> 60.9 us (0.927)
  Pallas kernels: 61.8 us -> 57 us
    pallas_call x1, Pallas kernels: 61.8 us -> 57 us  [on_device(): pl.pallas_call(kernel, out_shape=(jax.ShapeDtypeStruct((2, 2, W, W), F32)...]
where the time goes in v2:
time: 60.9 us; the launch traced here: 60.8 us
  Pallas kernels  57 us (94%)
  local copies, waits for them, and re-layouts  2.52 us (4%)
  between operations  1.29 us (2%)
    pallas_call x1, Pallas kernels, on_device(): pl.pallas_call(kernel, out_shape=(jax.ShapeDtypeStruct((2, 2, W, W), F32)...  57 us
    unnamed x4, local copies, waits for them, and re-layouts  2.52 us

profile of v2, /device:TPU:1, one launch (start us, length us, event | category | flops | bytes accessed | tf_op | source)
XLA Modules:
  0.0 60.8 jit_solution(16662714508415187256)
XLA Ops:
  1.3 57.0 %shard_map.77 = (f32[2,2,128,128]{3,2,1,0:T(8,128)}, f32[4,2,128,128]{3,2,1,0:T(8,128)}) custom-call(s32[2,4]{1,0:T(2,128)} %bitcast.3, s32[1,1]{1,0:T(1,128)S(6)} %copy.10.cnt, f32[2,2,128,128]{3,2,1,0:T(8,128)} %obj.1, f32[4,2,128,128]{3,2,1,0:T(8,128)} %probe_hbm.1, f32[4,128,128]{2,1,0:T(8,128)} %bitcast.2, bf16[4,2,256,256]{3,2,1,0:T(8,128)(2,1)} %constant.2.clone.tab_hbm), custom_call_target="tpu_custom_call" | custom-call | tf_op jit(solution)/shard_map/pallas_call | solution.py:467
  58.2 0.0 copy-start
  58.3 1.7 %copy.11 = f32[2,2,128,128]{3,2,1,0:T(8,128)} copy(f32[2,2,128,128]{3,2,1,0:T(8,128)} %get-tuple-element.4) | data formatting | bytes 524288
  60.0 0.0 copy-done
  60.0 0.8 %copy.12 = f32[4,2,128,128]{3,2,1,0:T(8,128)} copy(f32[4,2,128,128]{3,2,1,0:T(8,128)S(1)} %copy-done) | data formatting | bytes 1048576
Async XLA Ops:
  58.2 1.7 %copy-start = (f32[4,2,128,128]{3,2,1,0:T(8,128)S(1)}, f32[4,2,128,128]{3,2,1,0:T(8,128)}, u32[]{:S(2)}) copy-start(f32[4,2,128,128]{3,2,1,0:T(8,128)} %get-tuple-element.5) | copy-start | bytes 1572868

commit v3 on v2

--- a/solution.py
+++ b/solution.py
@@ -79,9 +79,9 @@
 
 
 def kernel(
-    off, cnt, obj, probe_hbm, meas_hbm, tab_hbm, gobj, gprobe,
+    off_hbm, cnt_hbm, obj, probe_hbm, meas_hbm, tab_hbm, gobj, gprobe,
     probe, meas, tab, ext0, ext1, win, tbuf, gt, gwin, pad, gext0, gext1, glow, gright, gside, gfar,
-    acc, rcore, rp, zb, res, lsem, ssem, rsem,
+    acc, rcore, rp, zb, res, off, cnt, lsem, ssem, rsem,
 ):
     ty, tx = lax.axis_index("ty"), lax.axis_index("tx")
     core, y, xh = lax.rem(ty, 2), lax.rem(lax.div(ty, 2), 4), lax.div(ty, 8)
@@ -98,6 +98,8 @@
         (probe_hbm, probe),
         (tab_hbm, tab),
         (meas_hbm, meas),
+        (off_hbm, off),
+        (cnt_hbm, cnt),
     ):
         local.append(pltpu.make_async_copy(src, dst, lsem.at[len(local)]))
         local[-1].start()
@@ -236,6 +238,8 @@
     local[2].wait()
     local[3].wait()
     local[4].wait()
+    local[5].wait()
+    local[6].wait()
     a_r, a_l, f_r, f_l = (tab.at[i] for i in range(4))
 
     halo_wait(0)
@@ -438,7 +442,7 @@
 
 
 def on_device(object_slices, probe, measured, offsets, counts):
-    smem, vmem, hbm = (pl.BlockSpec(memory_space=s) for s in (pltpu.SMEM, pltpu.VMEM, pl.ANY))
+    vmem, hbm = (pl.BlockSpec(memory_space=s) for s in (pltpu.VMEM, pl.ANY))
     shapes = [
         (MODES, 2, W, W),
         (SLOTS, W, W),
@@ -463,11 +467,12 @@
         (MODES, 2 * W, W),
     ]
     scratch = [pltpu.VMEM(s, F32) if s else pltpu.VMEM((4, 2, 2 * W, 2 * W), BF16) for s in shapes]
-    scratch += [pltpu.SemaphoreType.DMA((5,)), pltpu.SemaphoreType.DMA((COPIES,)), pltpu.SemaphoreType.DMA((COPIES,))]
+    scratch += [pltpu.SMEM((2, SLOTS), jnp.int32), pltpu.SMEM((1, 1), jnp.int32)]
+    scratch += [pltpu.SemaphoreType.DMA((7,)), pltpu.SemaphoreType.DMA((COPIES,)), pltpu.SemaphoreType.DMA((COPIES,))]
     return pl.pallas_call(
         kernel,
         out_shape=(jax.ShapeDtypeStruct((2, 2, W, W), F32), jax.ShapeDtypeStruct((MODES, 2, W, W), F32)),
-        in_specs=[smem, smem, hbm, hbm, hbm, hbm],
+        in_specs=[hbm] * 6,
         out_specs=(vmem, vmem),
         scratch_shapes=scratch,
         compiler_params=pltpu.CompilerParams(collective_id=0, has_side_effects=True),

time: 60.9 us -> 60.2 us (0.989)
  Pallas kernels: 57 us -> 56.3 us
    pallas_call x1, Pallas kernels: 57 us -> 56.3 us  [on_device(): pl.pallas_call(kernel, out_shape=(jax.ShapeDtypeStruct((2, 2, W, W), F32)...]
where the time goes in v3:
time: 60.2 us; the launch traced here: 60.1 us
  Pallas kernels  56.3 us (94%)
  local copies, waits for them, and re-layouts  2.52 us (4%)
  between operations  1.29 us (2%)
    pallas_call x1, Pallas kernels, on_device(): pl.pallas_call(kernel, out_shape=(jax.ShapeDtypeStruct((2, 2, W, W), F32)...  56.3 us
    unnamed x4, local copies, waits for them, and re-layouts  2.52 us

profile of v3, /device:TPU:1, one launch (start us, length us, event | category | flops | bytes accessed | tf_op | source)
XLA Modules:
  0.0 60.1 jit_solution(15618978455545141328)
XLA Ops:
  1.3 56.3 %shard_map.77 = (f32[2,2,128,128]{3,2,1,0:T(8,128)}, f32[4,2,128,128]{3,2,1,0:T(8,128)}) custom-call(s32[2,4]{1,0:T(2,128)} %bitcast.3, s32[1,1]{1,0:T(1,128)S(6)} %copy.10.cnt_hbm, f32[2,2,128,128]{3,2,1,0:T(8,128)} %obj.1, f32[4,2,128,128]{3,2,1,0:T(8,128)} %probe_hbm.1, f32[4,128,128]{2,1,0:T(8,128)} %bitcast.2, ...), custom_call_target="tpu_custom_call" | custom-call | tf_op jit(solution)/shard_map/pallas_call | solution.py:472
  57.6 0.0 copy-start
  57.6 1.7 %copy.11 = f32[2,2,128,128]{3,2,1,0:T(8,128)} copy(f32[2,2,128,128]{3,2,1,0:T(8,128)} %get-tuple-element.4) | data formatting | bytes 524288
  59.3 0.0 copy-done
  59.3 0.8 %copy.12 = f32[4,2,128,128]{3,2,1,0:T(8,128)} copy(f32[4,2,128,128]{3,2,1,0:T(8,128)S(1)} %copy-done) | data formatting | bytes 1048576
Async XLA Ops:
  57.6 1.7 %copy-start = (f32[4,2,128,128]{3,2,1,0:T(8,128)S(1)}, f32[4,2,128,128]{3,2,1,0:T(8,128)}, u32[]{:S(2)}) copy-start(f32[4,2,128,128]{3,2,1,0:T(8,128)} %get-tuple-element.5) | copy-start | bytes 1572868

commit v4 on v3

--- a/solution.py
+++ b/solution.py
@@ -373,12 +373,13 @@
             q = cmulc((win[0, s, 0], win[0, s, 1]), gu[s])
             total = q if total is None else add(total, q)
         acc[m, 0:W, :], acc[m, W : 2 * W, :] = total
+        if m == MODES - 2:
+            scatter_core(0)
         if m % 2 == 0:
             continue
         start(by_core[m - 1 : m + 1])
         if m == MODES - 1:
             send_far(1)
-            scatter_core(0)
 
     scatter_core(1)
     send_down(0)
@@ -438,6 +439,20 @@
                 copy.wait_send()
 
 
+def hand_over(gobj, gprobe, gobj_out, gprobe_out, gobj_held, gprobe_held, in_sem, out_sem):
+    parts = [(gobj, gobj_held, gobj_out, i) for i in range(2)]
+    parts += [(gprobe, gprobe_held, gprobe_out, i) for i in range(MODES)]
+    taken = [pltpu.make_async_copy(a.at[i], b.at[i], in_sem.at[k]) for k, (a, b, _, i) in enumerate(parts)]
+    given = [pltpu.make_async_copy(b.at[i], c.at[i], out_sem.at[k]) for k, (_, b, c, i) in enumerate(parts)]
+    for copy in taken:
+        copy.start()
+    for first, second in zip(taken, given, strict=True):
+        first.wait()
+        second.start()
+    for copy in given:
+        copy.wait()
+
+
 COPIES = 24 + MODES + 2 * 41
 
 
@@ -469,7 +484,7 @@
     scratch = [pltpu.VMEM(s, F32) if s else pltpu.VMEM((4, 2, 2 * W, 2 * W), BF16) for s in shapes]
     scratch += [pltpu.SMEM((2, SLOTS), jnp.int32), pltpu.SMEM((1, 1), jnp.int32)]
     scratch += [pltpu.SemaphoreType.DMA((7,)), pltpu.SemaphoreType.DMA((COPIES,)), pltpu.SemaphoreType.DMA((COPIES,))]
-    return pl.pallas_call(
+    grads = pl.pallas_call(
         kernel,
         out_shape=(jax.ShapeDtypeStruct((2, 2, W, W), F32), jax.ShapeDtypeStruct((MODES, 2, W, W), F32)),
         in_specs=[hbm] * 6,
@@ -479,6 +494,19 @@
     )(
         offsets.reshape(2, SLOTS), counts, object_slices, probe, measured.reshape(SLOTS, W, W), jnp.asarray(tables())
     )
+    pieces = 2 + MODES
+    return pl.pallas_call(
+        hand_over,
+        out_shape=tuple(jax.ShapeDtypeStruct(g.shape, F32) for g in grads),
+        in_specs=[hbm, hbm],
+        out_specs=(hbm, hbm),
+        scratch_shapes=[
+            pltpu.VMEM(grads[0].shape, F32),
+            pltpu.VMEM(grads[1].shape, F32),
+            pltpu.SemaphoreType.DMA((pieces,)),
+            pltpu.SemaphoreType.DMA((pieces,)),
+        ],
+    )(*grads)
 
 
 def solution(mesh):

time: 60.2 us -> 59.5 us (0.988)
  local copies, waits for them, and re-layouts: 2.52 us -> 0 us
  Pallas kernels: 56.3 us -> 58.2 us
    unnamed x4 -> x0, local copies, waits for them, and re-layouts: 2.52 us -> none
    pallas_call x0 -> x1, Pallas kernels: none -> 1.97 us  [on_device(): pl.pallas_call(hand_over, out_shape=tuple((jax.ShapeDtypeStruct(g.shape,...]
where the time goes in v4:
time: 59.5 us; the launch traced here: 59.4 us
  Pallas kernels  58.2 us (98%)
  between operations  1.29 us (2%)
    pallas_call x1, Pallas kernels, on_device(): pl.pallas_call(kernel, out_shape=(jax.ShapeDtypeStruct((2, 2, W, W), F32)...  56.2 us
    pallas_call x1, Pallas kernels, on_device(): pl.pallas_call(hand_over, out_shape=tuple((jax.ShapeDtypeStruct(g.shape,...  1.97 us

profile of v4, /device:TPU:1, one launch (start us, length us, event | category | flops | bytes accessed | tf_op | source)
XLA Modules:
  0.0 59.4 jit_solution(5496409828232957064)
XLA Ops:
  1.3 56.2 %shard_map.77 = (f32[2,2,128,128]{3,2,1,0:T(8,128)}, f32[4,2,128,128]{3,2,1,0:T(8,128)}) custom-call(s32[2,4]{1,0:T(2,128)} %bitcast.3, s32[1,1]{1,0:T(1,128)S(6)} %copy.8.cnt_hbm, f32[2,2,128,128]{3,2,1,0:T(8,128)} %obj.1, f32[4,2,128,128]{3,2,1,0:T(8,128)} %probe_hbm.1, f32[4,128,128]{2,1,0:T(8,128)} %bitcast.2, bf16[4,2,256,256]{3,2,1,0:T(8,128)(2,1)} %constant.2.clone.tab_hbm), custom_call_target="tpu_custom_call" | custom-call | tf_op jit(solution)/shard_map/pallas_call | solution.py:487
  57.5 2.0 %shard_map.78 = (f32[2,2,128,128]{3,2,1,0:T(8,128)}, f32[4,2,128,128]{3,2,1,0:T(8,128)}) custom-call(f32[2,2,128,128]{3,2,1,0:T(8,128)} %get-tuple-element.4.gobj, f32[4,2,128,128]{3,2,1,0:T(8,128)} %get-tuple-element.5.gprobe), custom_call_target="tpu_custom_call" | custom-call | tf_op jit(solution)/shard_map/pallas_call | solution.py:498
